TPU v7x, 128 devices: a whole 4x4x4 slice. The times are simulated.
128 devices in a mesh: dp: 8 (over z, core), tensor: 16 (over x, y).
Axes of the slice: x: 4, y: 4, z: 4, core: 2. Of those that a mesh axis runs over, the one named last changes fastest.
Arguments:
- grad_codes: bfloat16 [8, 1024, 14, 1024], P(None, 'tensor', None, 'dp'), may hold values from -6 to 6
- grad_scales: bfloat16 [8, 1024, 14, 8], P(None, 'tensor', None, 'dp'), may hold values from 0.0099487305 to 0.19921875
- block_slot: int32 [112], replicated, may hold values from 0 to 111, as said below
- left_basis: bfloat16 [128, 1024, 1024], P(('dp', 'tensor')), may hold values from -0.1875 to 0.1875
- right_basis: bfloat16 [128, 1024, 1024], P(('dp', 'tensor')), may hold values from -0.1875 to 0.1875
- first_moment: bfloat16 [128, 1024, 1024], P(('dp', 'tensor')), may hold values from -0.119628906 to 0.119628906
- second_moment: bfloat16 [128, 1024, 1024], P(('dp', 'tensor')), may hold values from 9.9658966e-05 to 0.0099487305
- left_gram: bfloat16 [128, 1024, 1024], P(('dp', 'tensor')), may hold values from -0.59765625 to 0.59765625
- right_gram: bfloat16 [128, 1024, 1024], P(('dp', 'tensor')), may hold values from -0.59765625 to 0.59765625
Outputs:
- update: bfloat16 [8, 1024, 14, 1024], P(None, 'tensor', None, 'dp')
- first_moment_new: bfloat16 [128, 1024, 1024], P(('dp', 'tensor'))
- second_moment_new: bfloat16 [128, 1024, 1024], P(('dp', 'tensor'))
- left_gram_new: bfloat16 [128, 1024, 1024], P(('dp', 'tensor'))
- right_gram_new: bfloat16 [128, 1024, 1024], P(('dp', 'tensor'))
Inputs may be any that keep to these rules, and one draw needn't show every extreme that they name: `block_slot`: entries are distinct. Blocks are taken in an order drawn from the seed; the i-th goes to owner i mod 128, in its local slot i div 128, that is global slot (i mod 128) + i div 128.
All inputs are finite; a program needn't handle non-finite values.
Results may differ from a plain program's by a relative error of at most 0.0065.
Values may be sent and summed in bfloat16 or wider, within the bound.
A program may use at most 128 MiB of HBM per device.

v0:
```python
import jax
import jax.numpy as jnp
from jax import lax
from jax.sharding import PartitionSpec as P

beta_first = 0.9
beta_second = 0.95
gram_decay = 0.9
epsilon = 1e-08


def soap_block(
    gradient, left_basis, right_basis, first_moment, second_moment, left_gram, right_gram
):
    half = jnp.dot(left_basis.T, gradient, preferred_element_type=jnp.float32).astype(jnp.bfloat16)
    rotated = jnp.dot(half, right_basis, preferred_element_type=jnp.float32)
    moment_one = beta_first * first_moment.astype(jnp.float32) + (1.0 - beta_first) * rotated
    moment_two = (
        beta_second * second_moment.astype(jnp.float32) + (1.0 - beta_second) * rotated * rotated
    )
    direction = (moment_one / (jnp.sqrt(moment_two) + epsilon)).astype(jnp.bfloat16)
    half_back = jnp.dot(left_basis, direction, preferred_element_type=jnp.float32).astype(
        jnp.bfloat16
    )
    back = jnp.dot(half_back, right_basis.T, preferred_element_type=jnp.float32)
    left_new = gram_decay * left_gram.astype(jnp.float32) + (1.0 - gram_decay) * jnp.dot(
        gradient, gradient.T, preferred_element_type=jnp.float32
    )
    right_new = gram_decay * right_gram.astype(jnp.float32) + (1.0 - gram_decay) * jnp.dot(
        gradient.T, gradient, preferred_element_type=jnp.float32
    )
    return (
        back.astype(jnp.bfloat16),
        moment_one.astype(jnp.bfloat16),
        moment_two.astype(jnp.bfloat16),
        left_new.astype(jnp.bfloat16),
        right_new.astype(jnp.bfloat16),
    )


def on_device(
    grad_codes,
    grad_scales,
    block_slot,
    left_basis,
    right_basis,
    first_moment,
    second_moment,
    left_gram,
    right_gram,
):
    dp_count = lax.axis_size("dp")
    tensor_count = lax.axis_size("tensor")
    owners = dp_count * tensor_count
    slot_count = left_basis.shape[0]
    side = left_basis.shape[1]
    block_rows, tile_rows, block_cols, tile_cols = grad_codes.shape
    group_count = grad_scales.shape[3]
    group_width = tile_cols // group_count
    blocks_total = block_rows * block_cols
    chooser = (
        block_slot[None, :] == jnp.arange(owners * slot_count, dtype=jnp.int32)[:, None]
    ).astype(jnp.bfloat16)

    def pick(pieces):
        flat = pieces.reshape(blocks_total, -1)
        picked = jnp.dot(chooser, flat, preferred_element_type=jnp.float32).astype(jnp.bfloat16)
        return picked.reshape((owners, slot_count) + pieces.shape[1:])

    code_tiles = grad_codes.transpose(0, 2, 1, 3).reshape(blocks_total, tile_rows, tile_cols)
    scale_tiles = grad_scales.transpose(0, 2, 1, 3).reshape(blocks_total, tile_rows, group_count)
    scale_rows = scale_tiles.reshape(blocks_total, tile_rows * group_count)
    flat_shape = (owners, slot_count, tile_rows)
    code_part = pick(code_tiles)
    leading = code_part.shape[:-1]
    grouped = code_part.astype(jnp.float32).reshape(leading + (group_count, group_width))
    values_out = (
        grouped
        * pick(scale_rows).reshape(flat_shape + (group_count,)).astype(jnp.float32)[..., None]
    ).reshape(code_part.shape)
    received = lax.all_to_all(
        values_out.astype(jnp.bfloat16), ("dp", "tensor"), split_axis=0, concat_axis=0, tiled=True
    ).astype(values_out.dtype)
    gradient_blocks = received.astype(jnp.bfloat16).reshape(
        dp_count, tensor_count, slot_count, tile_rows, tile_cols
    )
    gradient_blocks = gradient_blocks.transpose(2, 1, 3, 0, 4).reshape(slot_count, side, side)
    results = [
        soap_block(
            gradient_blocks[0],
            left_basis[0],
            right_basis[0],
            first_moment[0],
            second_moment[0],
            left_gram[0],
            right_gram[0],
        )
    ]
    back_slots = jnp.stack([entry[0] for entry in results])
    moment_one = jnp.stack([entry[1] for entry in results])
    moment_two = jnp.stack([entry[2] for entry in results])
    left_new = jnp.stack([entry[3] for entry in results])
    right_new = jnp.stack([entry[4] for entry in results])
    outgoing_back = back_slots.reshape(
        slot_count, tensor_count, tile_rows, dp_count, tile_cols
    ).transpose(3, 1, 0, 2, 4)
    returned = lax.all_to_all(
        outgoing_back.reshape(owners, slot_count, tile_rows, tile_cols),
        ("dp", "tensor"),
        split_axis=0,
        concat_axis=0,
        tiled=True,
    )
    returned_flat = returned.reshape(owners * slot_count, tile_rows * tile_cols)
    placed = jnp.dot(chooser.T, returned_flat, preferred_element_type=jnp.float32).astype(
        jnp.bfloat16
    )
    placed = placed.reshape(block_rows, block_cols, tile_rows, tile_cols).transpose(0, 2, 1, 3)
    return (placed, moment_one, moment_two, left_new, right_new)


def solution(mesh):
    in_specs = (
        P(None, "tensor", None, "dp"),
        P(None, "tensor", None, "dp"),
        P(),
        P(("dp", "tensor"), None, None),
        P(("dp", "tensor"), None, None),
        P(("dp", "tensor"), None, None),
        P(("dp", "tensor"), None, None),
        P(("dp", "tensor"), None, None),
        P(("dp", "tensor"), None, None),
    )
    out_specs = (
        P(None, "tensor", None, "dp"),
        P(("dp", "tensor"), None, None),
        P(("dp", "tensor"), None, None),
        P(("dp", "tensor"), None, None),
        P(("dp", "tensor"), None, None),
    )
    return jax.shard_map(
        on_device, mesh=mesh, in_specs=in_specs, out_specs=out_specs, check_vma=False
    )
```

profile of v0, /device:TPU:1, one launch (start us, length us, event | category | flops | bytes accessed | tf_op | source)
XLA Modules:
  0.0 114.1 jit_solution(18302814134595220610)
XLA Ops:
  0.6 0.0 copy-start
  0.6 0.9 copy.22
  1.6 0.8 fusion.43
  2.4 0.1 copy.23
  2.5 3.0 %fusion.6 = f32[16,8,64,128]{3,1,2,0:T(8,128)S(1)} fusion(bf16[14,8,64,128]{3,2,1,0:T(8,128)(2,1)} %bitcast.124, s32[112]{0:T(128)} %param.11), kind=kOutput, calls=%fused_computation.14 | convolution fusion | flops 236992512 | bytes 6029760 | tf_op jit(solution)/shard_map/dot_general | solution.py:67
  5.5 0.7 copy.29
  6.3 1.5 %fusion.4 = bf16[128,1,64,128]{3,2,1,0:T(8,128)(2,1)S(1)} fusion(f32[128,64]{1,0:T(8,128)S(1)} %copy.23, f32[16,8,64,128]{3,2,1,0:T(8,128)S(1)} %copy.29), kind=kLoop, calls=%fused_computation.10 | loop fusion | flops 2097152 | bytes 6324224 | tf_op jit(solution)/shard_map/convert_element_type | solution.py:82
  7.8 41.1 %all_to_all.10 = bf16[128,1,64,128]{3,2,1,0:T(8,128)(2,1)S(1)} all-to-all(bf16[128,1,64,128]{3,2,1,0:T(8,128)(2,1)S(1)} %fusion.4), channel_id=1, replica_groups=mesh['dp'=8,'tensor'=16] {'dp','tensor'}, dimensions={0} | all-to-all | bytes 4194304 | tf_op jit(solution)/shard_map/all_to_all | solution.py:81
  48.9 3.1 %copy.25 = bf16[1,16,64,8,128]{4,3,2,1,0:T(8,128)(2,1)} copy(bf16[1,16,64,8,128]{4,2,1,3,0:T(8,128)(2,1)S(1)} %bitcast.118) | data formatting | bytes 4194304 | tf_op jit(solution)/shard_map/transpose | solution.py:87
  52.0 0.0 copy-done
  52.0 8.7 %fusion.18 = f32[1024,1024]{1,0:T(8,128)} fusion(bf16[1,1024,1024]{2,1,0:T(8,128)(2,1)} %param.13, bf16[1,1024,1024]{2,1,0:T(8,128)(2,1)S(1)} %copy-done, bf16[128,8,8,128]{3,2,1,0:T(8,128)(2,1)} %bitcast.120), kind=kOutput, calls=%fused_computation.26 | convolution fusion | flops 4296015872 | bytes 10485760 | tf_op jit(solution)/shard_map/dot_general | solution.py:16
  60.7 0.0 copy-start.3
  60.7 8.2 %fusion.20 = bf16[1024,1024]{1,0:T(8,128)(2,1)S(1)} fusion(bf16[1,1024,1024]{2,1,0:T(8,128)(2,1)S(1)} %copy-done, f32[1024,1024]{1,0:T(8,128)} %fusion.18, bf16[1,1024,1024]{2,1,0:T(8,128)(2,1)} %param.14, bf16[1,1024,1024]{2,1,0:T(8,128)(2,1)} %param.15), kind=kOutput, calls=%fused_computation.28 | convolution fusion | flops 2160066560 | bytes 12582912 | tf_op jit(solution)/shard_map/dot_general | solution.py:22
  68.9 0.0 copy-done.3
  68.9 2.6 %convert_bitcast_fusion = bf16[128,8,8,128]{3,1,2,0:T(8,128)(2,1)S(1)} fusion(bf16[1,1024,1024]{2,1,0:T(8,128)(2,1)S(1)} %copy-done.3, bf16[1024,1024]{1,0:T(8,128)(2,1)S(1)} %fusion.20), kind=kOutput, calls=%fused_computation.31 | convolution fusion | flops 2148532224 | bytes 6291456 | tf_op jit(solution)/shard_map/dot_general | solution.py:25
  71.6 0.6 copy.31
  72.2 1.9 %copy.26 = bf16[1,16,64,8,128]{4,2,1,3,0:T(8,128)(2,1)} copy(bf16[1,16,64,8,128]{4,3,2,1,0:T(8,128)(2,1)S(1)} %bitcast.119) | data formatting | bytes 4194304 | tf_op jit(solution)/shard_map/reshape;stack | solution.py:104
  74.1 5.5 %all-to-all-start.1 = ((bf16[128,1,64,128]{3,2,1,0:T(8,128)(2,1)}), bf16[128,1,64,128]{3,2,1,0:T(8,128)(2,1)}, u32[]{:S(2)}, u32[]{:S(2)}) async-start(bf16[128,1,64,128]{3,2,1,0:T(8,128)(2,1)} %bitcast.117), calls=%async_computation.1 | async-start | bytes 4194304 | tf_op jit(solution)/shard_map/all_to_all | solution.py:107
  79.6 0.0 copy-start.1
  79.7 0.0 copy-start.4
  79.7 7.2 %fusion.8 = (bf16[1,1024,1024]{2,1,0:T(8,128)(2,1)}, bf16[1,1024,1024]{2,1,0:T(8,128)(2,1)}) fusion(f32[1024,1024]{1,0:T(8,128)} %fusion.18, bf16[1,1024,1024]{2,1,0:T(8,128)(2,1)} %param.15, bf16[1,1024,1024]{2,1,0:T(8,128)(2,1)} %param.14), kind=kLoop, calls=%fused_computation.16 | loop fusion | flops 11534336 | bytes 12582912 | tf_op jit(solution)/shard_map/stack | solution.py:101
  86.8 0.0 copy-done.1
  86.8 0.0 copy-done.4
  86.8 0.0 copy-start.5
  86.8 3.7 %fusion.31 = bf16[1,1024,1024]{2,1,0:T(8,128)(2,1)} fusion(bf16[1,1024,1024]{2,1,0:T(8,128)(2,1)S(1)} %copy-done.4, bf16[128,8,8,128]{3,2,1,0:T(8,128)(2,1)S(1)} %bitcast.121), kind=kOutput, calls=%fused_computation.36 | convolution fusion | flops 2152726528 | bytes 6291456 | tf_op jit(solution)/shard_map/dot_general | solution.py:26
  90.6 0.0 copy-done.5
  90.6 0.0 copy-start.2
  90.6 4.0 %fusion.34 = bf16[1,1024,1024]{2,1,0:T(8,128)(2,1)} fusion(bf16[1,1024,1024]{2,1,0:T(8,128)(2,1)S(1)} %copy-done.5, bf16[128,8,8,128]{3,2,1,0:T(8,128)(2,1)S(1)} %bitcast.122), kind=kOutput, calls=%fused_computation.37 | convolution fusion | flops 2152726528 | bytes 6291456 | tf_op jit(solution)/shard_map/dot_general | solution.py:29
  94.5 14.6 %all-to-all-done.1 = bf16[128,1,64,128]{3,2,1,0:T(8,128)(2,1)} async-done(((bf16[128,1,64,128]{3,2,1,0:T(8,128)(2,1)}), bf16[128,1,64,128]{3,2,1,0:T(8,128)(2,1)}, u32[]{:S(2)}, u32[]{:S(2)}) %all-to-all-start.1) | async-done | bytes 2097184 | tf_op jit(solution)/shard_map/all_to_all | solution.py:107
  109.2 0.0 copy-done.2
  109.2 3.2 %fusion.40 = bf16[14,8,64,128]{3,1,2,0:T(8,128)(2,1)S(1)} fusion(bf16[16,8,64,128]{3,2,1,0:T(8,128)(2,1)} %bitcast.37, s32[112]{0:T(128)S(1)} %copy-done.2), kind=kOutput, calls=%fused_computation.41 | convolution fusion | flops 235812864 | bytes 3932608 | tf_op jit(solution)/shard_map/dot_general | solution.py:115
  112.4 1.7 %copy.33 = bf16[14,8,64,128]{3,2,1,0:T(8,128)(2,1)} copy(bf16[14,8,64,128]{3,1,2,0:T(8,128)(2,1)S(1)} %fusion.40) | data formatting | bytes 3670016
  (1 shorter events, 0.0 us)
Async XLA Ops:
  0.6 51.4 %copy-start = (bf16[1,1024,1024]{2,1,0:T(8,128)(2,1)S(1)}, bf16[1,1024,1024]{2,1,0:T(8,128)(2,1)}, u32[]{:S(2)}) copy-start(bf16[1,1024,1024]{2,1,0:T(8,128)(2,1)} %param.12) | copy-start | bytes 6291460
  60.7 8.2 %copy-start.3 = (bf16[1,1024,1024]{2,1,0:T(8,128)(2,1)S(1)}, bf16[1,1024,1024]{2,1,0:T(8,128)(2,1)}, u32[]{:S(2)}) copy-start(bf16[1,1024,1024]{2,1,0:T(8,128)(2,1)} %param.13) | copy-start | bytes 6291460
  74.1 35.1 %all-to-all-start.1 = ((bf16[128,1,64,128]{3,2,1,0:T(8,128)(2,1)}), bf16[128,1,64,128]{3,2,1,0:T(8,128)(2,1)}, u32[]{:S(2)}, u32[]{:S(2)}) async-start(bf16[128,1,64,128]{3,2,1,0:T(8,128)(2,1)} %bitcast.117), calls=%async_computation.1 | async-start | bytes 4194304 | tf_op jit(solution)/shard_map/all_to_all | solution.py:107
  79.6 7.2 %copy-start.1 = (bf16[1,16,64,8,128]{4,3,2,1,0:T(8,128)(2,1)S(1)}, bf16[1,16,64,8,128]{4,3,2,1,0:T(8,128)(2,1)}, u32[]{:S(2)}) copy-start(bf16[1,16,64,8,128]{4,3,2,1,0:T(8,128)(2,1)} %copy.25) | copy-start | bytes 6291460
  79.7 7.2 %copy-start.4 = (bf16[1,1024,1024]{2,1,0:T(8,128)(2,1)S(1)}, bf16[1,1024,1024]{2,1,0:T(8,128)(2,1)}, u32[]{:S(2)}) copy-start(bf16[1,1024,1024]{2,1,0:T(8,128)(2,1)} %param.16) | copy-start | bytes 6291460
  86.8 3.7 %copy-start.5 = (bf16[1,1024,1024]{2,1,0:T(8,128)(2,1)S(1)}, bf16[1,1024,1024]{2,1,0:T(8,128)(2,1)}, u32[]{:S(2)}) copy-start(bf16[1,1024,1024]{2,1,0:T(8,128)(2,1)} %param.17) | copy-start | bytes 6291460
  90.6 18.6 %copy-start.2 = (s32[112]{0:T(128)S(1)}, s32[112]{0:T(128)}, u32[]{:S(2)}) copy-start(s32[112]{0:T(128)} %param.11) | copy-start | bytes 1348
where the time goes:
time: 114 us
  blocking collectives  41.1 us (36%)
  matrix products  34.2 us (30%)
  waiting for transfers between devices  14.6 us (13%)
  local copies, waits for them, and re-layouts  9.2 us (8%)
  other arithmetic  8.69 us (8%)
  starting transfers between devices  5.51 us (5%)
    all_to_all x1, blocking collectives, on_device(): lax.all_to_all(values_out.astype(jnp.bfloat16), ('dp', 'tensor'), split_a...  41.1 us
    all_to_all x1, waiting for transfers between devices, on_device(): lax.all_to_all(outgoing_back.reshape(owners, slot_count, tile_rows, tile_...  14.6 us
    dot_general x1, matrix products, soap_block(): rotated = jnp.dot(half, right_basis, preferred_element_type=jnp.float32)  8.74 us
    dot_general x1, matrix products, soap_block(): jnp.dot(left_basis, direction, preferred_element_type=jnp.float32)  8.18 us
    another operation x1, other arithmetic, on_device(): moment_two = jnp.stack([entry[2] for entry in results])  7.17 us
    all_to_all x1, starting transfers between devices, on_device(): lax.all_to_all(outgoing_back.reshape(owners, slot_count, tile_rows, tile_...  5.51 us
    dot_general x1, matrix products, soap_block(): jnp.dot(gradient.T, gradient, preferred_element_type=jnp.float32)  3.96 us
    dot_general x2, matrix products, pick(): jnp.dot(chooser, flat, preferred_element_type=jnp.float32)  3.84 us
  transfers between devices with their start and end apart: 1, of which 1 were waited for; matrix products, arithmetic and copies ran while one was open for 13% of the time, Pallas kernels for 0%

commit v1 on v0

v1 whole, which is shorter than its diff:
```python
import functools

import jax
import jax.numpy as jnp
from jax import lax
from jax.experimental import pallas as pl
from jax.experimental.pallas import tpu as pltpu
from jax.sharding import PartitionSpec as P

beta_first = 0.9
beta_second = 0.95
gram_decay = 0.9
epsilon = 1e-08

CHUNK = 256
SLICE = 16


def nt(a, b):
    return lax.dot_general(a, b, (((1,), (1,)), ((), ())), preferred_element_type=jnp.float32)


def nn(a, b):
    return jnp.dot(a, b, preferred_element_type=jnp.float32)


def digits(i, *sizes):
    out = []
    for n in sizes:
        out.append(lax.rem(i, n))
        i = i // n
    return out


def kernel(
    inverse,
    slots,
    codes_hbm,
    scales,
    left_hbm,
    right_hbm,
    first_hbm,
    second_hbm,
    lgram_hbm,
    rgram_hbm,
    update_out,
    first_out,
    second_out,
    lgram_out,
    rgram_out,
    codes,
    stage,
    grad,
    flip,
    left,
    left_t,
    right,
    first,
    second,
    lgram,
    rgram,
    half,
    rotated,
    direction,
    back,
    arrived,
    load_sem,
    out_sem,
    grad_send,
    grad_recv,
    back_send,
    back_recv,
):
    blocks, tile_rows, tile_cols = codes.shape
    side = grad.shape[0]
    dp_index = lax.axis_index("dp")
    t_index = lax.axis_index("tensor")
    z, c = dp_index // 2, lax.rem(dp_index, 2)
    x, y = t_index // 4, lax.rem(t_index, 4)
    me = dp_index * 16 + t_index
    owner = me < blocks

    barrier = pltpu.get_barrier_semaphore()

    @pl.loop(1, 128)
    def _(i):
        o = lax.rem(me + i, 128)
        pl.semaphore_signal(
            barrier, inc=1, device_id={"dp": o // 16, "tensor": lax.rem(o, 16)}
        )

    loads = [
        pltpu.make_async_copy(src, dst, load_sem.at[n])
        for n, (src, dst) in enumerate(
            (
                (codes_hbm, codes),
                (left_hbm, left),
                (right_hbm, right),
                (first_hbm, first),
                (second_hbm, second),
                (lgram_hbm, lgram),
                (rgram_hbm, rgram),
            )
        )
    ]
    for copy in loads:
        copy.start()

    eye = (
        lax.broadcasted_iota(jnp.int32, (tile_rows, tile_rows), 0)
        == lax.broadcasted_iota(jnp.int32, (tile_rows, tile_rows), 1)
    ).astype(jnp.bfloat16)
    scale_t = nt(eye, scales[...])
    lane = lax.broadcasted_iota(jnp.int32, (tile_rows, blocks), 1)
    lane_block = lax.rem(lane, 8) * 14 + lane // 8

    def tile_at(ref, o):
        rows = pl.multiple_of(lax.rem(o, 16) * tile_rows, tile_rows)
        cols = pl.multiple_of((o // 16) * tile_cols, tile_cols)
        return ref.at[pl.ds(rows, tile_rows), pl.ds(cols, tile_cols)]

    loads[0].wait()
    pl.semaphore_wait(barrier, 127)

    @pl.loop(0, 128)
    def _(i):
        dzb, a, b, zp, core = digits(i, 2, 4, 4, 2, 2)
        z2 = lax.rem(z + 2 * dzb + 1 - zp, 4)
        x2 = lax.rem(x + a, 4)
        y2 = lax.rem(y + a + b, 4)
        o = (z2 * 2 + core) * 16 + x2 * 4 + y2

        @pl.when(o < blocks)
        def _():
            block = inverse[o]
            scale = jnp.sum(
                jnp.where(lane_block == block, scale_t, 0.0), axis=1, keepdims=True
            )
            stage[o] = (codes[block].astype(jnp.float32) * scale).astype(jnp.bfloat16)

            @pl.when(o != me)
            def _():
                pltpu.make_async_remote_copy(
                    stage.at[o],
                    tile_at(grad, me),
                    grad_send,
                    grad_recv,
                    device_id={"dp": z2 * 2 + core, "tensor": x2 * 4 + y2},
                ).start()

    @pl.when(owner)
    def _():
        pltpu.sync_copy(stage.at[me], tile_at(grad, me))

    @pl.when(jnp.logical_not(owner))
    def _():
        grad[...] = jnp.zeros_like(grad)

    def chunked(body):
        @pl.loop(0, side // CHUNK)
        def _(i):
            body(pl.ds(pl.multiple_of(i * CHUNK, CHUNK), CHUNK))

    loads[1].wait()

    def flip_left(rows):
        left_t[rows, :] = left[:, rows].T

    chunked(flip_left)
    for copy in loads[2:]:
        copy.wait()

    @pl.when(owner)
    def _():
        pltpu.make_async_copy(
            arrived_bytes(arrived, 127), arrived_bytes(arrived, 127), grad_recv
        ).wait()

    def to_direction(rows):
        half_rows = nn(left_t[rows, :], grad[...]).astype(jnp.bfloat16)
        rotated[...] = nn(half_rows, right[...])

        @pl.loop(0, CHUNK // SLICE)
        def _(j):
            inner = pl.ds(pl.multiple_of(j * SLICE, SLICE), SLICE)
            outer = pl.ds(pl.multiple_of(rows.start + j * SLICE, SLICE), SLICE)
            turned = rotated[inner, :]
            m = beta_first * first[outer, :].astype(jnp.float32) + (1.0 - beta_first) * turned
            v = (
                beta_second * second[outer, :].astype(jnp.float32)
                + (1.0 - beta_second) * turned * turned
            )
            direction[outer, :] = (m / (jnp.sqrt(v) + epsilon)).astype(jnp.bfloat16)
            first[outer, :] = m.astype(jnp.bfloat16)
            second[outer, :] = v.astype(jnp.bfloat16)

    chunked(to_direction)
    stores = [
        pltpu.make_async_copy(first, first_out, out_sem.at[0]),
        pltpu.make_async_copy(second, second_out, out_sem.at[1]),
        pltpu.make_async_copy(lgram, lgram_out, out_sem.at[2]),
        pltpu.make_async_copy(rgram, rgram_out, out_sem.at[3]),
        pltpu.make_async_copy(codes, update_out, out_sem.at[4]),
    ]
    stores[0].start()
    stores[1].start()

    for parity in (1, 0):

        @pl.loop(0, 2)
        def _(k):
            x2 = lax.rem(x + 2 * k + parity, 4)
            rows = pl.ds(pl.multiple_of(x2 * CHUNK, CHUNK), CHUNK)
            half[...] = nn(left[rows, :], direction[...]).astype(jnp.bfloat16)
            back[rows, :] = nt(half[...], right[...]).astype(jnp.bfloat16)

        @pl.when(owner)
        def _():
            @pl.loop(0, 64)
            def _(i):
                dzb, k, dyb, core, zp, yp = digits(i, 2, 2, 2, 2, 2, 2)
                z2 = lax.rem(z + 2 * dzb + 1 - zp, 4)
                x2 = lax.rem(x + 2 * k + parity, 4)
                y2 = lax.rem(y + 2 * dyb + yp, 4)
                o = (z2 * 2 + core) * 16 + x2 * 4 + y2

                @pl.when(o != me)
                def _():
                    pltpu.make_async_remote_copy(
                        tile_at(back, o),
                        arrived.at[me],
                        back_send,
                        back_recv,
                        device_id={"dp": z2 * 2 + core, "tensor": x2 * 4 + y2},
                    ).start()

    @pl.when(owner)
    def _():
        pltpu.sync_copy(tile_at(back, me), arrived.at[me])

    def flip_grad(rows):
        flip[rows, :] = grad[:, rows].T

    chunked(flip_grad)

    def grams(rows):
        lgram[rows, :] = (
            gram_decay * lgram[rows, :].astype(jnp.float32)
            + (1.0 - gram_decay) * nt(grad[rows, :], grad[...])
        ).astype(jnp.bfloat16)
        rgram[rows, :] = (
            gram_decay * rgram[rows, :].astype(jnp.float32)
            + (1.0 - gram_decay) * nt(flip[rows, :], flip[...])
        ).astype(jnp.bfloat16)

    chunked(grams)
    stores[2].start()
    stores[3].start()

    @pl.when(owner)
    def _():
        pltpu.make_async_copy(
            arrived_bytes(arrived, 111), arrived_bytes(arrived, 111), back_recv
        ).wait()

    @pl.when(jnp.logical_not(owner))
    def _():
        pltpu.make_async_copy(
            arrived_bytes(arrived, 112), arrived_bytes(arrived, 112), back_recv
        ).wait()

    @pl.loop(0, blocks)
    def _(b):
        codes[b] = arrived[slots[b]]

    stores[4].start()

    @pl.when(owner)
    def _():
        pltpu.make_async_copy(
            arrived_bytes(arrived, 111), arrived_bytes(arrived, 111), grad_send
        ).wait()
        pltpu.make_async_copy(
            arrived_bytes(arrived, 127), arrived_bytes(arrived, 127), back_send
        ).wait()

    @pl.when(jnp.logical_not(owner))
    def _():
        pltpu.make_async_copy(
            arrived_bytes(arrived, 112), arrived_bytes(arrived, 112), grad_send
        ).wait()

    for copy in stores:
        copy.wait()


def arrived_bytes(ref, tiles):
    return ref.at[pl.ds(0, tiles)]


def on_device(
    grad_codes,
    grad_scales,
    block_slot,
    left_basis,
    right_basis,
    first_moment,
    second_moment,
    left_gram,
    right_gram,
):
    block_rows, tile_rows, block_cols, tile_cols = grad_codes.shape
    blocks = block_rows * block_cols
    side = left_basis.shape[1]
    bf16 = jnp.bfloat16
    order = jnp.arange(blocks, dtype=jnp.int32)
    inverse = jnp.sum(
        jnp.where(block_slot[None, :] == order[:, None], order[None, :], 0), axis=1
    )
    codes = grad_codes.transpose(0, 2, 1, 3).reshape(blocks, tile_rows, tile_cols)
    scales = grad_scales.transpose(2, 3, 0, 1).reshape(blocks, tile_rows)
    square = (side, side)
    anywhere = pl.BlockSpec(memory_space=pl.ANY)
    outs = pl.pallas_call(
        kernel,
        name="soap_exchange",
        out_shape=[jax.ShapeDtypeStruct((blocks, tile_rows, tile_cols), bf16)]
        + [jax.ShapeDtypeStruct(square, bf16)] * 4,
        in_specs=[
            pl.BlockSpec(memory_space=pltpu.SMEM),
            pl.BlockSpec(memory_space=pltpu.SMEM),
            anywhere,
            pl.BlockSpec(memory_space=pltpu.VMEM),
        ]
        + [anywhere] * 6,
        out_specs=[anywhere] * 5,
        scratch_shapes=[
            pltpu.VMEM((blocks, tile_rows, tile_cols), bf16),
            pltpu.VMEM((blocks, tile_rows, tile_cols), bf16),
        ]
        + [pltpu.VMEM(square, bf16)] * 9
        + [
            pltpu.VMEM((CHUNK, side), bf16),
            pltpu.VMEM((CHUNK, side), jnp.float32),
            pltpu.VMEM(square, bf16),
            pltpu.VMEM(square, bf16),
            pltpu.VMEM((128, tile_rows, tile_cols), bf16),
            pltpu.SemaphoreType.DMA((7,)),
            pltpu.SemaphoreType.DMA((5,)),
            pltpu.SemaphoreType.DMA,
            pltpu.SemaphoreType.DMA,
            pltpu.SemaphoreType.DMA,
            pltpu.SemaphoreType.DMA,
        ],
        compiler_params=pltpu.CompilerParams(
            collective_id=0, has_side_effects=True, vmem_limit_bytes=56 << 20
        ),
    )(
        inverse,
        block_slot,
        codes,
        scales,
        left_basis[0],
        right_basis[0],
        first_moment[0],
        second_moment[0],
        left_gram[0],
        right_gram[0],
    )
    update = outs[0].reshape(block_rows, block_cols, tile_rows, tile_cols)
    return (update.transpose(0, 2, 1, 3),) + tuple(a[None] for a in outs[1:])


def solution(mesh):
    whole = P(("dp", "tensor"), None, None)
    tiles = P(None, "tensor", None, "dp")
    return jax.shard_map(
        on_device,
        mesh=mesh,
        in_specs=(tiles, tiles, P()) + (whole,) * 6,
        out_specs=(tiles,) + (whole,) * 4,
        check_vma=False,
    )
```

time: 114 us -> 91.6 us (0.80)
  Pallas kernels: 0 us -> 78 us
  blocking collectives: 41.1 us -> 0 us
  matrix products: 34.2 us -> 0 us
  waiting for transfers between devices: 14.6 us -> 0 us
  other arithmetic: 8.69 us -> 1.29 us
  starting transfers between devices: 5.51 us -> 0 us
  local copies, waits for them, and re-layouts: 9.2 us -> 11.4 us
    pallas_call x0 -> x1, Pallas kernels: none -> 78 us  [on_device(): pl.pallas_call(kernel, name='soap_exchange', out_shape=[jax.ShapeDtypeStr...]
    all_to_all x1 -> x0, blocking collectives: 41.1 us -> none  [on_device(): lax.all_to_all(values_out.astype(jnp.bfloat16), ('dp', 'tensor'), split_a...]
    dot_general x8 -> x0, matrix products: 34.2 us -> none  [the longest x1 8.74 us: soap_block(): rotated = jnp.dot(half, right_basis, preferred_element_type=jnp.float32)]
    all_to_all x1 -> x0, waiting for transfers between devices: 14.6 us -> none  [on_device(): lax.all_to_all(outgoing_back.reshape(owners, slot_count, tile_rows, tile_...]
    unnamed x15 -> x13, local copies, waits for them, and re-layouts: 3.14 us -> 11.4 us
    another operation x1 -> x0, other arithmetic: 7.17 us -> none  [on_device(): moment_two = jnp.stack([entry[2] for entry in results])]
    all_to_all x1 -> x0, starting transfers between devices: 5.51 us -> none  [on_device(): lax.all_to_all(outgoing_back.reshape(owners, slot_count, tile_rows, tile_...]
    transpose x2 -> x0, local copies, waits for them, and re-layouts: 4.02 us -> none  [the longest x1 3.12 us: on_device(): gradient_blocks.transpose(2, 1, 3, 0, 4).reshape(slot_count, side, side)]
  transfers between devices with their start and end apart: 1 -> 0, of which waited for: 1 -> 0; matrix products, arithmetic and copies ran while one was open for 13% -> 0% of each run, Pallas kernels for 0% -> 0%
where the time goes in v1:
time: 91.6 us; the launch traced here: 91.3 us
  Pallas kernels  78 us (85%)
  local copies, waits for them, and re-layouts  11.4 us (12%)
  other arithmetic  1.29 us (1%)
    pallas_call x1, Pallas kernels, on_device(): pl.pallas_call(kernel, name='soap_exchange', out_shape=[jax.ShapeDtypeStr...  78 us
    unnamed x13, local copies, waits for them, and re-layouts  11.4 us

profile of v1, /device:TPU:1, one launch (start us, length us, event | category | flops | bytes accessed | tf_op | source)
XLA Modules:
  0.0 91.3 jit_solution(16284622947066884919)
XLA Ops:
  0.6 1.3 %select_reduce_fusion.inverse = s32[112]{0:T(128)} fusion(s32[112]{0:T(128)} %slots.1), kind=kLoop, calls=%fused_computation | loop fusion | flops 37520 | bytes 896 | tf_op jit(solution)/shard_map/reduce_sum | solution.py:317
  1.9 78.0 %soap_exchange.1 = (bf16[112,64,128]{2,1,0:T(8,128)(2,1)}, bf16[1024,1024]{1,0:T(8,128)(2,1)}, bf16[1024,1024]{1,0:T(8,128)(2,1)}, bf16[1024,1024]{1,0:T(8,128)(2,1)}, bf16[1024,1024]{1,0:T(8,128)(2,1)}) custom-call(s32[112]{0:T(128)} %select_reduce_fusion.inverse, s32[112]{0:T(128)} %slots.1, bf16[112,64,128]{2,1,0:T(8,128)(2,1)} %bitcast.29, ...), custom_call_target="tpu_custom_call" | custom-call | tf_op jit(solution)/shard_map/soap_exchange/pallas_call | solution.py:324
  79.9 0.0 copy-start.3
  79.9 3.0 %copy.19 = bf16[8,64,14,128]{3,1,2,0:T(8,128)(2,1)} copy(bf16[8,64,14,128]{3,1,2,0:T(8,128)(2,1)} %bitcast.30) | data formatting | bytes 3670016
  83.0 0.0 copy-done.3
  83.0 0.0 copy-start.2
  83.0 1.3 %copy.20 = bf16[1,1024,1024]{2,1,0:T(8,128)(2,1)} copy(bf16[1,1024,1024]{2,1,0:T(8,128)(2,1)S(1)} %bitcast.28) | data formatting | bytes 4194304
  84.3 1.0 %copy-done.2 = bf16[1024,1024]{1,0:T(8,128)(2,1)S(1)} copy-done((bf16[1024,1024]{1,0:T(8,128)(2,1)S(1)}, bf16[1024,1024]{1,0:T(8,128)(2,1)}, u32[]{:S(2)}) %copy-start.2) | copy-done | bytes 2097176
  85.3 0.0 copy-start.1
  85.3 1.3 %copy.21 = bf16[1,1024,1024]{2,1,0:T(8,128)(2,1)} copy(bf16[1,1024,1024]{2,1,0:T(8,128)(2,1)S(1)} %bitcast.27) | data formatting | bytes 4194304
  86.6 1.0 %copy-done.1 = bf16[1024,1024]{1,0:T(8,128)(2,1)S(1)} copy-done((bf16[1024,1024]{1,0:T(8,128)(2,1)S(1)}, bf16[1024,1024]{1,0:T(8,128)(2,1)}, u32[]{:S(2)}) %copy-start.1) | copy-done | bytes 2097176
  87.7 0.0 copy-start
  87.7 1.3 %copy.22 = bf16[1,1024,1024]{2,1,0:T(8,128)(2,1)} copy(bf16[1,1024,1024]{2,1,0:T(8,128)(2,1)S(1)} %bitcast.26) | data formatting | bytes 4194304
  89.0 1.0 %copy-done = bf16[1024,1024]{1,0:T(8,128)(2,1)S(1)} copy-done((bf16[1024,1024]{1,0:T(8,128)(2,1)S(1)}, bf16[1024,1024]{1,0:T(8,128)(2,1)}, u32[]{:S(2)}) %copy-start) | copy-done | bytes 2097176
  90.0 1.3 %copy.23 = bf16[1,1024,1024]{2,1,0:T(8,128)(2,1)} copy(bf16[1,1024,1024]{2,1,0:T(8,128)(2,1)S(1)} %bitcast.25) | data formatting | bytes 4194304
Async XLA Ops:
  79.9 3.0 %copy-start.3 = (bf16[1024,1024]{1,0:T(8,128)(2,1)S(1)}, bf16[1024,1024]{1,0:T(8,128)(2,1)}, u32[]{:S(2)}) copy-start(bf16[1024,1024]{1,0:T(8,128)(2,1)} %get-tuple-element.11) | copy-start | bytes 6291460
  83.0 2.3 %copy-start.2 = (bf16[1024,1024]{1,0:T(8,128)(2,1)S(1)}, bf16[1024,1024]{1,0:T(8,128)(2,1)}, u32[]{:S(2)}) copy-start(bf16[1024,1024]{1,0:T(8,128)(2,1)} %get-tuple-element.12) | copy-start | bytes 6291460
  85.3 2.3 %copy-start.1 = (bf16[1024,1024]{1,0:T(8,128)(2,1)S(1)}, bf16[1024,1024]{1,0:T(8,128)(2,1)}, u32[]{:S(2)}) copy-start(bf16[1024,1024]{1,0:T(8,128)(2,1)} %get-tuple-element.13) | copy-start | bytes 6291460
  87.7 2.3 %copy-start = (bf16[1024,1024]{1,0:T(8,128)(2,1)S(1)}, bf16[1024,1024]{1,0:T(8,128)(2,1)}, u32[]{:S(2)}) copy-start(bf16[1024,1024]{1,0:T(8,128)(2,1)} %get-tuple-element.14) | copy-start | bytes 6291460

commit v2 on v1

v2 whole, which is shorter than its diff:
```python
import functools

import jax
import jax.numpy as jnp
from jax import lax
from jax.experimental import pallas as pl
from jax.experimental.pallas import tpu as pltpu
from jax.sharding import PartitionSpec as P

beta_first = 0.9
beta_second = 0.95
gram_decay = 0.9
epsilon = 1e-08

CHUNK = 256
SLICE = 16
PART = 128


def nt(a, b):
    return lax.dot_general(a, b, (((1,), (1,)), ((), ())), preferred_element_type=jnp.float32)


def nn(a, b):
    return jnp.dot(a, b, preferred_element_type=jnp.float32)


def digits(i, *sizes):
    out = []
    for n in sizes:
        out.append(lax.rem(i, n))
        i = i // n
    return out


def kernel(
    slots_hbm,
    codes_hbm,
    scales_hbm,
    left_hbm,
    right_hbm,
    first_hbm,
    second_hbm,
    lgram_hbm,
    rgram_hbm,
    arrived,
    first_new,
    second_new,
    lgram_new,
    rgram_new,
    slots,
    scales,
    table,
    inverse,
    codes,
    stage,
    grad,
    flip,
    left,
    left_t,
    right,
    first,
    second,
    lgram,
    rgram,
    half,
    direction,
    back,
    rotated,
    turned_even,
    turned_odd,
    half_back,
    load_sem,
    table_sem,
    grad_send,
    grad_recv,
    back_send,
    back_recv,
):
    blocks, tile_rows, tile_cols = codes.shape
    side = grad.shape[0]
    dp_index = lax.axis_index("dp")
    t_index = lax.axis_index("tensor")
    z = dp_index // 2
    x, y = t_index // 4, lax.rem(t_index, 4)
    me = dp_index * 16 + t_index
    owner = me < blocks

    loads = [
        pltpu.make_async_copy(src, dst, load_sem.at[n])
        for n, (src, dst) in enumerate(
            (
                (slots_hbm, slots),
                (scales_hbm, scales),
                (codes_hbm, codes),
                (left_hbm, left),
                (right_hbm, right),
                (first_hbm, first),
                (second_hbm, second),
                (lgram_hbm, lgram),
                (rgram_hbm, rgram),
            )
        )
    ]
    for copy in loads[:3]:
        copy.start()

    barrier = pltpu.get_barrier_semaphore()

    def greet(i):
        o = lax.rem(me + i, 128)
        pl.semaphore_signal(
            barrier, inc=1, device_id={"dp": o // 16, "tensor": lax.rem(o, 16)}
        )

    @pl.loop(1, 72)
    def _(i):
        greet(i)

    loads[0].wait()
    down = lax.broadcasted_iota(jnp.int32, (blocks, blocks), 0)
    across = lax.broadcasted_iota(jnp.int32, (blocks, blocks), 1)
    column = jnp.sum(jnp.where(down == across, slots[...], 0), axis=1, keepdims=True)
    table[...] = jnp.max(jnp.where(column == across, down, 0), axis=0, keepdims=True)
    fetch = pltpu.make_async_copy(table, inverse, table_sem)
    fetch.start()

    loads[1].wait()
    eye = (
        lax.broadcasted_iota(jnp.int32, (tile_rows, tile_rows), 0)
        == lax.broadcasted_iota(jnp.int32, (tile_rows, tile_rows), 1)
    ).astype(jnp.bfloat16)
    scale_t = nt(eye, scales[...])
    lane = lax.broadcasted_iota(jnp.int32, (tile_rows, blocks), 1)
    lane_block = lax.rem(lane, 8) * 14 + lane // 8

    def tile_at(ref, o):
        rows = pl.multiple_of(lax.rem(o, 16) * tile_rows, tile_rows)
        cols = pl.multiple_of((o // 16) * tile_cols, tile_cols)
        return ref.at[pl.ds(rows, tile_rows), pl.ds(cols, tile_cols)]

    fetch.wait()
    loads[2].wait()
    for copy in loads[3:]:
        copy.start()

    @pl.loop(0, blocks // 4)
    def _(i):
        greet(72 + 2 * i)
        greet(73 + 2 * i)
        for q in range(4):
            o = 4 * i + q
            block = inverse[0, o]
            scale = jnp.sum(
                jnp.where(lane_block == block, scale_t, 0.0), axis=1, keepdims=True
            )
            stage[o] = (codes[block].astype(jnp.float32) * scale).astype(jnp.bfloat16)

    pl.semaphore_wait(barrier, 127)

    @pl.loop(0, 128)
    def _(i):
        dzb, a, b, zp, core = digits(i, 2, 4, 4, 2, 2)
        z2 = lax.rem(z + 2 * dzb + 1 - zp, 4)
        x2 = lax.rem(x + a, 4)
        y2 = lax.rem(y + a + b, 4)
        o = (z2 * 2 + core) * 16 + x2 * 4 + y2

        @pl.when(jnp.logical_and(o < blocks, o != me))
        def _():
            pltpu.make_async_remote_copy(
                stage.at[o],
                tile_at(grad, me),
                grad_send,
                grad_recv.at[zp],
                device_id={"dp": z2 * 2 + core, "tensor": x2 * 4 + y2},
            ).start()

    @pl.when(owner)
    def _():
        pltpu.sync_copy(stage.at[me], tile_at(grad, me))

    @pl.when(jnp.logical_not(owner))
    def _():
        grad[...] = jnp.zeros_like(grad)

    def chunked(body):
        @pl.loop(0, side // CHUNK)
        def _(i):
            body(pl.ds(pl.multiple_of(i * CHUNK, CHUNK), CHUNK))

    loads[3].wait()

    def flip_left(rows):
        left_t[rows, :] = left[:, rows].T

    chunked(flip_left)
    for copy in loads[4:]:
        copy.wait()

    def span(k):
        return pl.ds(pl.multiple_of(lax.rem(z + k, 4) * CHUNK, CHUNK), CHUNK)

    def to_half(k):
        half[:, span(k)] = nn(left_t[...], grad[:, span(k)]).astype(jnp.bfloat16)

    def turn(rows, k):
        return nn(half[rows, span(k)], right[span(k), :])

    @pl.when(owner)
    def _():
        wait_tiles(arrived, 64, grad_recv.at[0])

    to_half(1)
    to_half(3)

    def turn_first(rows):
        rotated[rows, :] = turn(rows, 1) + turn(rows, 3)

    chunked(turn_first)

    @pl.when(owner)
    def _():
        wait_tiles(arrived, 63, grad_recv.at[1])

    to_half(2)
    to_half(0)

    def step(rows, turned):
        m = beta_first * first[rows, :].astype(jnp.float32) + (1.0 - beta_first) * turned
        v = (
            beta_second * second[rows, :].astype(jnp.float32)
            + (1.0 - beta_second) * turned * turned
        )
        root = v * lax.rsqrt(v)
        direction[rows, :] = (m / (root + epsilon)).astype(jnp.bfloat16)
        first_new[rows, :] = m.astype(jnp.bfloat16)
        second_new[rows, :] = v.astype(jnp.bfloat16)

    parts = side // PART
    for i in range(parts + 1):
        if i < parts:
            rows = pl.ds(i * PART, PART)
            turned = turned_odd if i % 2 else turned_even
            turned[...] = rotated[rows, :] + turn(rows, 2) + turn(rows, 0)
        if i > 0:
            turned = turned_even if i % 2 else turned_odd
            for j in range(PART // SLICE):
                step(
                    pl.ds((i - 1) * PART + j * SLICE, SLICE),
                    turned[pl.ds(j * SLICE, SLICE), :],
                )

    for parity in (1, 0):

        @pl.loop(0, 2)
        def _(k):
            x2 = lax.rem(x + 2 * k + parity, 4)
            rows = pl.ds(pl.multiple_of(x2 * CHUNK, CHUNK), CHUNK)
            half_back[...] = nn(left[rows, :], direction[...]).astype(jnp.bfloat16)
            back[rows, :] = nt(half_back[...], right[...]).astype(jnp.bfloat16)

        @pl.when(owner)
        def _():
            @pl.loop(0, 64)
            def _(i):
                dzb, k, dyb, core, zp, yp = digits(i, 2, 2, 2, 2, 2, 2)
                z2 = lax.rem(z + 2 * dzb + 1 - zp, 4)
                x2 = lax.rem(x + 2 * k + parity, 4)
                y2 = lax.rem(y + 2 * dyb + yp, 4)
                o = (z2 * 2 + core) * 16 + x2 * 4 + y2

                @pl.when(o != me)
                def _():
                    pltpu.make_async_remote_copy(
                        tile_at(back, o),
                        arrived.at[me],
                        back_send,
                        back_recv,
                        device_id={"dp": z2 * 2 + core, "tensor": x2 * 4 + y2},
                    ).start()

    @pl.when(owner)
    def _():
        pltpu.sync_copy(tile_at(back, me), arrived.at[me])

    def flip_grad(rows):
        flip[rows, :] = grad[:, rows].T

    chunked(flip_grad)

    def grams(rows):
        lgram_new[rows, :] = (
            gram_decay * lgram[rows, :].astype(jnp.float32)
            + (1.0 - gram_decay) * nt(grad[rows, :], grad[...])
        ).astype(jnp.bfloat16)
        rgram_new[rows, :] = (
            gram_decay * rgram[rows, :].astype(jnp.float32)
            + (1.0 - gram_decay) * nt(flip[rows, :], flip[...])
        ).astype(jnp.bfloat16)

    chunked(grams)

    @pl.when(owner)
    def _():
        wait_tiles(arrived, 111, grad_send)
        wait_tiles(arrived, 127, back_send)
        wait_tiles(arrived, 111, back_recv)

    @pl.when(jnp.logical_not(owner))
    def _():
        wait_tiles(arrived, 112, grad_send)
        wait_tiles(arrived, 112, back_recv)


def wait_tiles(ref, tiles, sem):
    part = ref.at[pl.ds(0, tiles)]
    pltpu.make_async_copy(part, part, sem).wait()


def publish(slots, arrived, *refs):
    kept, update, made, tile_sem, sems = refs[:4], refs[4], refs[5:9], refs[9], refs[10]
    copies = [
        pltpu.make_async_copy(a, b, sems.at[n]) for n, (a, b) in enumerate(zip(kept, made))
    ]
    for copy in copies:
        copy.start()

    @pl.loop(0, update.shape[0])
    def _(b):
        pltpu.make_async_copy(arrived.at[slots[b]], update.at[b], tile_sem).start()

    every = arrived.at[pl.ds(0, update.shape[0])]
    pltpu.make_async_copy(every, update, tile_sem).wait()
    for copy in copies:
        copy.wait()


def on_device(
    grad_codes,
    grad_scales,
    block_slot,
    left_basis,
    right_basis,
    first_moment,
    second_moment,
    left_gram,
    right_gram,
):
    block_rows, tile_rows, block_cols, tile_cols = grad_codes.shape
    blocks = block_rows * block_cols
    side = left_basis.shape[1]
    bf16 = jnp.bfloat16
    codes = grad_codes.transpose(0, 2, 1, 3).reshape(blocks, tile_rows, tile_cols)
    scales = grad_scales.transpose(2, 3, 0, 1).reshape(blocks, tile_rows)
    held = [
        pltpu.with_memory_space_constraint(a, pltpu.HBM)
        for a in (
            block_slot.reshape(1, blocks),
            codes,
            scales,
            left_basis[0],
            right_basis[0],
            first_moment[0],
            second_moment[0],
            left_gram[0],
            right_gram[0],
        )
    ]
    square = (side, side)
    anywhere = pl.BlockSpec(memory_space=pltpu.HBM)
    outs = pl.pallas_call(
        kernel,
        name="soap_exchange",
        out_shape=[pltpu.VMEM((128, tile_rows, tile_cols), bf16)]
        + [pltpu.VMEM(square, bf16)] * 4,
        in_specs=[anywhere] * 9,
        out_specs=[pl.BlockSpec(memory_space=pltpu.VMEM)] * 5,
        scratch_shapes=[
            pltpu.VMEM((1, blocks), jnp.int32),
            pltpu.VMEM((blocks, tile_rows), bf16),
            pltpu.VMEM((1, blocks), jnp.int32),
            pltpu.SMEM((1, blocks), jnp.int32),
            pltpu.VMEM((blocks, tile_rows, tile_cols), bf16),
            pltpu.VMEM((blocks, tile_rows, tile_cols), bf16),
        ]
        + [pltpu.VMEM(square, bf16)] * 12
        + [
            pltpu.VMEM(square, jnp.float32),
            pltpu.VMEM((PART, side), jnp.float32),
            pltpu.VMEM((PART, side), jnp.float32),
            pltpu.VMEM((CHUNK, side), bf16),
            pltpu.SemaphoreType.DMA((9,)),
            pltpu.SemaphoreType.DMA,
            pltpu.SemaphoreType.DMA,
            pltpu.SemaphoreType.DMA((2,)),
            pltpu.SemaphoreType.DMA,
            pltpu.SemaphoreType.DMA,
        ],
        compiler_params=pltpu.CompilerParams(
            collective_id=0, has_side_effects=True, vmem_limit_bytes=40 << 20
        ),
    )(*held)
    outs = pl.pallas_call(
        publish,
        name="publish",
        out_shape=[jax.ShapeDtypeStruct(codes.shape, bf16)]
        + [jax.ShapeDtypeStruct(square, bf16)] * 4,
        in_specs=[pl.BlockSpec(memory_space=pltpu.SMEM)]
        + [pl.BlockSpec(memory_space=pltpu.VMEM)] * 5,
        out_specs=[pl.BlockSpec(memory_space=pltpu.HBM)] * 5,
        scratch_shapes=[pltpu.SemaphoreType.DMA, pltpu.SemaphoreType.DMA((4,))],
        compiler_params=pltpu.CompilerParams(vmem_limit_bytes=1 << 20),
    )(block_slot, *[pltpu.with_memory_space_constraint(a, pltpu.VMEM) for a in outs])
    update = outs[0].reshape(block_rows, block_cols, tile_rows, tile_cols)
    return (update.transpose(0, 2, 1, 3),) + tuple(a[None] for a in outs[1:])


def solution(mesh):
    whole = P(("dp", "tensor"), None, None)
    tiles = P(None, "tensor", None, "dp")
    return jax.shard_map(
        on_device,
        mesh=mesh,
        in_specs=(tiles, tiles, P()) + (whole,) * 6,
        out_specs=(tiles,) + (whole,) * 4,
        check_vma=False,
    )
```

time: 91.6 us -> 71.7 us (0.78)
  local copies, waits for them, and re-layouts: 11.4 us -> 0.01 us
  Pallas kernels: 78 us -> 70.9 us
  other arithmetic: 1.29 us -> 0 us
    unnamed x13 -> x2, local copies, waits for them, and re-layouts: 11.4 us -> 0.01 us
    pallas_call x1 -> x2, Pallas kernels: 78 us -> 70.9 us  [the longest x1 66.5 us: on_device(): pl.pallas_call(kernel, name='soap_exchange', out_shape=[pltpu.VMEM((128,...]
    reduce_sum x1 -> x0, other arithmetic: 1.29 us -> none  [on_device(): jnp.sum(jnp.where(block_slot[None, :] == order[:, None], order[None, :],...]
where the time goes in v2:
time: 71.7 us; the launch traced here: 71.5 us
  Pallas kernels  70.9 us (99%)
    pallas_call x1, Pallas kernels, on_device(): pl.pallas_call(kernel, name='soap_exchange', out_shape=[pltpu.VMEM((128,...  66.5 us
    pallas_call x1, Pallas kernels, on_device(): pl.pallas_call(publish, name='publish', out_shape=[jax.ShapeDtypeStruct(c...  4.36 us

profile of v2, /device:TPU:1, one launch (start us, length us, event | category | flops | bytes accessed | tf_op | source)
XLA Modules:
  0.0 71.5 jit_solution(12444498635620093216)
XLA Ops:
  0.6 0.0 copy-start
  0.6 66.5 %soap_exchange.1 = (bf16[128,64,128]{2,1,0:T(8,128)(2,1)S(1)}, bf16[1024,1024]{1,0:T(8,128)(2,1)S(1)}, bf16[1024,1024]{1,0:T(8,128)(2,1)S(1)}, bf16[1024,1024]{1,0:T(8,128)(2,1)S(1)}, bf16[1024,1024]{1,0:T(8,128)(2,1)S(1)}) custom-call(s32[1,112]{1,0:T(1,128)} %bitcast.20, bf16[112,64,128]{2,1,0:T(8,128)(2,1)} %bitcast.27, bf16[112,64]{1,0:T(8,128)(2,1)} %bitcast.28, ...), custom_call_target="tpu_custom_call" | custom-call | tf_op jit(solution)/shard_map/soap_exchange/pallas_call | solution.py:372
  67.2 0.0 copy-done
  67.2 4.4 %publish.1 = (bf16[112,64,128]{2,1,0:T(8,128)(2,1)}, bf16[1024,1024]{1,0:T(8,128)(2,1)}, bf16[1024,1024]{1,0:T(8,128)(2,1)}, bf16[1024,1024]{1,0:T(8,128)(2,1)}, bf16[1024,1024]{1,0:T(8,128)(2,1)}) custom-call(s32[112]{0:T(128)S(1)} %copy-done, bf16[128,64,128]{2,1,0:T(8,128)(2,1)S(1)} %get-tuple-element.15.arrived, ...), custom_call_target="tpu_custom_call" | custom-call | tf_op jit(solution)/shard_map/publish/pallas_call | solution.py:404
Async XLA Ops:
  0.6 66.5 %copy-start = (s32[112]{0:T(128)S(1)}, s32[112]{0:T(128)}, u32[]{:S(2)}) copy-start(s32[112]{0:T(128)} %slots.1) | copy-start | bytes 1348

commit v3 on v2

--- a/solution.py
+++ b/solution.py
@@ -81,7 +81,7 @@
     side = grad.shape[0]
     dp_index = lax.axis_index("dp")
     t_index = lax.axis_index("tensor")
-    z = dp_index // 2
+    z, c = dp_index // 2, lax.rem(dp_index, 2)
     x, y = t_index // 4, lax.rem(t_index, 4)
     me = dp_index * 16 + t_index
     owner = me < blocks
@@ -113,7 +113,7 @@
             barrier, inc=1, device_id={"dp": o // 16, "tensor": lax.rem(o, 16)}
         )
 
-    @pl.loop(1, 72)
+    @pl.loop(1, 128)
     def _(i):
         greet(i)
 
@@ -146,8 +146,6 @@
 
     @pl.loop(0, blocks // 4)
     def _(i):
-        greet(72 + 2 * i)
-        greet(73 + 2 * i)
         for q in range(4):
             o = 4 * i + q
             block = inverse[0, o]
@@ -232,8 +230,8 @@
             beta_second * second[rows, :].astype(jnp.float32)
             + (1.0 - beta_second) * turned * turned
         )
-        root = v * lax.rsqrt(v)
-        direction[rows, :] = (m / (root + epsilon)).astype(jnp.bfloat16)
+        root = v * lax.rsqrt(v) + epsilon
+        direction[rows, :] = (m * lax.rsqrt(root * root)).astype(jnp.bfloat16)
         first_new[rows, :] = m.astype(jnp.bfloat16)
         second_new[rows, :] = v.astype(jnp.bfloat16)
 
@@ -251,22 +249,34 @@
                     turned[pl.ds(j * SLICE, SLICE), :],
                 )
 
-    for parity in (1, 0):
-
-        @pl.loop(0, 2)
-        def _(k):
-            x2 = lax.rem(x + 2 * k + parity, 4)
-            rows = pl.ds(pl.multiple_of(x2 * CHUNK, CHUNK), CHUNK)
-            half_back[...] = nn(left[rows, :], direction[...]).astype(jnp.bfloat16)
-            back[rows, :] = nt(half_back[...], right[...]).astype(jnp.bfloat16)
+    @pl.loop(0, 4)
+    def _(turn_at):
+        yp, even = lax.rem(turn_at, 2), turn_at // 2
+        places = [
+            pl.multiple_of(
+                lax.rem(x + 2 * k + 1 - even, 4) * CHUNK
+                + lax.rem(y + 2 * dyb + yp, 4) * tile_rows,
+                tile_rows,
+            )
+            for k in range(2)
+            for dyb in range(2)
+        ]
+        picked = [left[pl.ds(p, tile_rows), :] for p in places]
+        half_back[...] = nn(jnp.concatenate(picked, axis=0), direction[...]).astype(
+            jnp.bfloat16
+        )
+        out = nt(half_back[...], right[...]).astype(jnp.bfloat16)
+        for n, p in enumerate(places):
+            back[pl.ds(p, tile_rows), :] = out[n * tile_rows : (n + 1) * tile_rows]
 
         @pl.when(owner)
         def _():
-            @pl.loop(0, 64)
+            @pl.loop(0, 32)
             def _(i):
-                dzb, k, dyb, core, zp, yp = digits(i, 2, 2, 2, 2, 2, 2)
-                z2 = lax.rem(z + 2 * dzb + 1 - zp, 4)
-                x2 = lax.rem(x + 2 * k + parity, 4)
+                core, dzb, k, dyb, zp = digits(i, 2, 2, 2, 2, 2)
+                core = lax.rem(core + c, 2)
+                z2 = lax.rem(z + 2 * (dzb + c) + 1 - zp, 4)
+                x2 = lax.rem(x + 2 * k + 1 - even, 4)
                 y2 = lax.rem(y + 2 * dyb + yp, 4)
                 o = (z2 * 2 + core) * 16 + x2 * 4 + y2
 

time: 71.7 us -> 69.7 us (0.972)
  Pallas kernels: 70.9 us -> 68.9 us
    pallas_call x1, Pallas kernels: 66.5 us -> 64.6 us  [on_device(): pl.pallas_call(kernel, name='soap_exchange', out_shape=[pltpu.VMEM((128,...]
where the time goes in v3:
time: 69.7 us; the launch traced here: 69.6 us
  Pallas kernels  68.9 us (99%)
    pallas_call x1, Pallas kernels, on_device(): pl.pallas_call(kernel, name='soap_exchange', out_shape=[pltpu.VMEM((128,...  64.6 us
    pallas_call x1, Pallas kernels, on_device(): pl.pallas_call(publish, name='publish', out_shape=[jax.ShapeDtypeStruct(c...  4.36 us

profile of v3, /device:TPU:1, one launch (start us, length us, event | category | flops | bytes accessed | tf_op | source)
XLA Modules:
  0.0 69.6 jit_solution(6241942808472729384)
XLA Ops:
  0.6 0.0 copy-start
  0.6 64.6 %soap_exchange.1 = (bf16[128,64,128]{2,1,0:T(8,128)(2,1)S(1)}, bf16[1024,1024]{1,0:T(8,128)(2,1)S(1)}, bf16[1024,1024]{1,0:T(8,128)(2,1)S(1)}, bf16[1024,1024]{1,0:T(8,128)(2,1)S(1)}, bf16[1024,1024]{1,0:T(8,128)(2,1)S(1)}) custom-call(s32[1,112]{1,0:T(1,128)} %bitcast.20, bf16[112,64,128]{2,1,0:T(8,128)(2,1)} %bitcast.27, bf16[112,64]{1,0:T(8,128)(2,1)} %bitcast.28, ...), custom_call_target="tpu_custom_call" | custom-call | tf_op jit(solution)/shard_map/soap_exchange/pallas_call | solution.py:382
  65.2 0.0 copy-done
  65.2 4.4 %publish.1 = (bf16[112,64,128]{2,1,0:T(8,128)(2,1)}, bf16[1024,1024]{1,0:T(8,128)(2,1)}, bf16[1024,1024]{1,0:T(8,128)(2,1)}, bf16[1024,1024]{1,0:T(8,128)(2,1)}, bf16[1024,1024]{1,0:T(8,128)(2,1)}) custom-call(s32[112]{0:T(128)S(1)} %copy-done, bf16[128,64,128]{2,1,0:T(8,128)(2,1)S(1)} %get-tuple-element.15.arrived, ...), custom_call_target="tpu_custom_call" | custom-call | tf_op jit(solution)/shard_map/publish/pallas_call | solution.py:414
Async XLA Ops:
  0.6 64.6 %copy-start = (s32[112]{0:T(128)S(1)}, s32[112]{0:T(128)}, u32[]{:S(2)}) copy-start(s32[112]{0:T(128)} %slots.1) | copy-start | bytes 1348

commit v4 on v3

--- a/solution.py
+++ b/solution.py
@@ -113,9 +113,12 @@
             barrier, inc=1, device_id={"dp": o // 16, "tensor": lax.rem(o, 16)}
         )
 
-    @pl.loop(1, 128)
+    @pl.loop(0, 18)
     def _(i):
-        greet(i)
+        for q in range(7):
+            greet(1 + 7 * i + q)
+
+    greet(127)
 
     loads[0].wait()
     down = lax.broadcasted_iota(jnp.int32, (blocks, blocks), 0)
@@ -232,6 +235,14 @@
         )
         root = v * lax.rsqrt(v) + epsilon
         direction[rows, :] = (m * lax.rsqrt(root * root)).astype(jnp.bfloat16)
+
+    def keep(rows):
+        turned = rotated[rows, :]
+        m = beta_first * first[rows, :].astype(jnp.float32) + (1.0 - beta_first) * turned
+        v = (
+            beta_second * second[rows, :].astype(jnp.float32)
+            + (1.0 - beta_second) * turned * turned
+        )
         first_new[rows, :] = m.astype(jnp.bfloat16)
         second_new[rows, :] = v.astype(jnp.bfloat16)
 
@@ -239,14 +250,12 @@
     for i in range(parts + 1):
         if i < parts:
             rows = pl.ds(i * PART, PART)
-            turned = turned_odd if i % 2 else turned_even
-            turned[...] = rotated[rows, :] + turn(rows, 2) + turn(rows, 0)
+            rotated[rows, :] = rotated[rows, :] + turn(rows, 2) + turn(rows, 0)
         if i > 0:
-            turned = turned_even if i % 2 else turned_odd
             for j in range(PART // SLICE):
                 step(
                     pl.ds((i - 1) * PART + j * SLICE, SLICE),
-                    turned[pl.ds(j * SLICE, SLICE), :],
+                    rotated[pl.ds((i - 1) * PART + j * SLICE, SLICE), :],
                 )
 
     @pl.loop(0, 4)
@@ -293,6 +302,10 @@
     @pl.when(owner)
     def _():
         pltpu.sync_copy(tile_at(back, me), arrived.at[me])
+
+    @pl.loop(0, side // SLICE)
+    def _(i):
+        keep(pl.ds(pl.multiple_of(i * SLICE, SLICE), SLICE))
 
     def flip_grad(rows):
         flip[rows, :] = grad[:, rows].T

time: 69.7 us -> 69 us (0.990)
  Pallas kernels: 68.9 us -> 68.2 us
where the time goes in v4:
time: 69 us; the launch traced here: 68.9 us
  Pallas kernels  68.2 us (99%)
    pallas_call x1, Pallas kernels, on_device(): pl.pallas_call(kernel, name='soap_exchange', out_shape=[pltpu.VMEM((128,...  63.9 us
    pallas_call x1, Pallas kernels, on_device(): pl.pallas_call(publish, name='publish', out_shape=[jax.ShapeDtypeStruct(c...  4.36 us

profile of v4, /device:TPU:1, one launch (start us, length us, event | category | flops | bytes accessed | tf_op | source)
XLA Modules:
  0.0 68.9 jit_solution(14951028202509099576)
XLA Ops:
  0.6 0.0 copy-start
  0.6 63.9 %soap_exchange.1 = (bf16[128,64,128]{2,1,0:T(8,128)(2,1)S(1)}, bf16[1024,1024]{1,0:T(8,128)(2,1)S(1)}, bf16[1024,1024]{1,0:T(8,128)(2,1)S(1)}, bf16[1024,1024]{1,0:T(8,128)(2,1)S(1)}, bf16[1024,1024]{1,0:T(8,128)(2,1)S(1)}) custom-call(s32[1,112]{1,0:T(1,128)} %bitcast.20, bf16[112,64,128]{2,1,0:T(8,128)(2,1)} %bitcast.27, bf16[112,64]{1,0:T(8,128)(2,1)} %bitcast.28, ...), custom_call_target="tpu_custom_call" | custom-call | tf_op jit(solution)/shard_map/soap_exchange/pallas_call | solution.py:395
  64.5 0.0 copy-done
  64.5 4.4 %publish.1 = (bf16[112,64,128]{2,1,0:T(8,128)(2,1)}, bf16[1024,1024]{1,0:T(8,128)(2,1)}, bf16[1024,1024]{1,0:T(8,128)(2,1)}, bf16[1024,1024]{1,0:T(8,128)(2,1)}, bf16[1024,1024]{1,0:T(8,128)(2,1)}) custom-call(s32[112]{0:T(128)S(1)} %copy-done, bf16[128,64,128]{2,1,0:T(8,128)(2,1)S(1)} %get-tuple-element.15.arrived, ...), custom_call_target="tpu_custom_call" | custom-call | tf_op jit(solution)/shard_map/publish/pallas_call | solution.py:427
Async XLA Ops:
  0.6 63.9 %copy-start = (s32[112]{0:T(128)S(1)}, s32[112]{0:T(128)}, u32[]{:S(2)}) copy-start(s32[112]{0:T(128)} %slots.1) | copy-start | bytes 1348

commit v5 on v4

--- a/solution.py
+++ b/solution.py
@@ -258,9 +258,9 @@
                     rotated[pl.ds((i - 1) * PART + j * SLICE, SLICE), :],
                 )
 
-    @pl.loop(0, 4)
+    @pl.loop(0, 8)
     def _(turn_at):
-        yp, even = lax.rem(turn_at, 2), turn_at // 2
+        dyb, yp, even = digits(turn_at, 2, 2, 2)
         places = [
             pl.multiple_of(
                 lax.rem(x + 2 * k + 1 - even, 4) * CHUNK
@@ -268,7 +268,6 @@
                 tile_rows,
             )
             for k in range(2)
-            for dyb in range(2)
         ]
         picked = [left[pl.ds(p, tile_rows), :] for p in places]
         half_back[...] = nn(jnp.concatenate(picked, axis=0), direction[...]).astype(
@@ -280,9 +279,9 @@
 
         @pl.when(owner)
         def _():
-            @pl.loop(0, 32)
+            @pl.loop(0, 16)
             def _(i):
-                core, dzb, k, dyb, zp = digits(i, 2, 2, 2, 2, 2)
+                core, dzb, k, zp = digits(i, 2, 2, 2, 2)
                 core = lax.rem(core + c, 2)
                 z2 = lax.rem(z + 2 * (dzb + c) + 1 - zp, 4)
                 x2 = lax.rem(x + 2 * k + 1 - even, 4)
@@ -412,7 +411,7 @@
             pltpu.VMEM(square, jnp.float32),
             pltpu.VMEM((PART, side), jnp.float32),
             pltpu.VMEM((PART, side), jnp.float32),
-            pltpu.VMEM((CHUNK, side), bf16),
+            pltpu.VMEM((PART, side), bf16),
             pltpu.SemaphoreType.DMA((9,)),
             pltpu.SemaphoreType.DMA,
             pltpu.SemaphoreType.DMA,

time: 69 us -> 71.4 us (1.035)
  Pallas kernels: 68.2 us -> 70.6 us
    pallas_call x1, Pallas kernels: 63.9 us -> 66.2 us  [on_device(): pl.pallas_call(kernel, name='soap_exchange', out_shape=[pltpu.VMEM((128,...]
where the time goes in v5:
time: 71.4 us; the launch traced here: 71.3 us
  Pallas kernels  70.6 us (99%)
    pallas_call x1, Pallas kernels, on_device(): pl.pallas_call(kernel, name='soap_exchange', out_shape=[pltpu.VMEM((128,...  66.2 us
    pallas_call x1, Pallas kernels, on_device(): pl.pallas_call(publish, name='publish', out_shape=[jax.ShapeDtypeStruct(c...  4.36 us

profile of v5, /device:TPU:1, one launch (start us, length us, event | category | flops | bytes accessed | tf_op | source)
XLA Modules:
  0.0 71.3 jit_solution(8216829069665345249)
XLA Ops:
  0.6 0.0 copy-start
  0.6 66.2 %soap_exchange.1 = (bf16[128,64,128]{2,1,0:T(8,128)(2,1)S(1)}, bf16[1024,1024]{1,0:T(8,128)(2,1)S(1)}, bf16[1024,1024]{1,0:T(8,128)(2,1)S(1)}, bf16[1024,1024]{1,0:T(8,128)(2,1)S(1)}, bf16[1024,1024]{1,0:T(8,128)(2,1)S(1)}) custom-call(s32[1,112]{1,0:T(1,128)} %bitcast.20, bf16[112,64,128]{2,1,0:T(8,128)(2,1)} %bitcast.27, bf16[112,64]{1,0:T(8,128)(2,1)} %bitcast.28, ...), custom_call_target="tpu_custom_call" | custom-call | tf_op jit(solution)/shard_map/soap_exchange/pallas_call | solution.py:394
  66.9 0.0 copy-done
  66.9 4.4 %publish.1 = (bf16[112,64,128]{2,1,0:T(8,128)(2,1)}, bf16[1024,1024]{1,0:T(8,128)(2,1)}, bf16[1024,1024]{1,0:T(8,128)(2,1)}, bf16[1024,1024]{1,0:T(8,128)(2,1)}, bf16[1024,1024]{1,0:T(8,128)(2,1)}) custom-call(s32[112]{0:T(128)S(1)} %copy-done, bf16[128,64,128]{2,1,0:T(8,128)(2,1)S(1)} %get-tuple-element.15.arrived, ...), custom_call_target="tpu_custom_call" | custom-call | tf_op jit(solution)/shard_map/publish/pallas_call | solution.py:426
Async XLA Ops:
  0.6 66.3 %copy-start = (s32[112]{0:T(128)S(1)}, s32[112]{0:T(128)}, u32[]{:S(2)}) copy-start(s32[112]{0:T(128)} %slots.1) | copy-start | bytes 1348
